TPU v7x, 256 devices: a whole 4x4x8 slice. The times are simulated.
256 devices in a mesh: fsdp: 64 (over y, z, core), tp: 4 (over x).
Axes of the slice: x: 4, y: 4, z: 8, core: 2. Of those that a mesh axis runs over, the one named last changes fastest.
Arguments:
- grads: float32 [4, 512, 256, 256], P('tp', None, 'fsdp'), may hold values from -200 to 200
- weights: float32 [512, 256, 256], P('tp', 'fsdp'), may hold values from -0.3 to 0.3
- moments: float32 [512, 256, 256], P('tp', 'fsdp'), may hold values from 0.05 to 2
- left_stat: float32 [4, 64, 6, 256, 256], P('tp', 'fsdp'), may hold values from -20 to 200
- right_stat: float32 [4, 64, 6, 256, 256], P('tp', 'fsdp'), may hold values from -20 to 200
- left_root: bfloat16 [4, 64, 6, 256, 256], P('tp', 'fsdp'), may hold values from -1 to 2
- right_root: bfloat16 [4, 64, 6, 256, 256], P('tp', 'fsdp'), may hold values from -1 to 2
- owner: int32 [512], P('tp'), may hold values from 0 to 63, as said below
- extent: int32 [512, 2], P('tp'), may hold values from 1 to 2
Outputs:
- new_weights: float32 [512, 256, 256], P('tp', 'fsdp')
- new_moments: float32 [512, 256, 256], P('tp', 'fsdp')
- new_left: float32 [4, 64, 6, 256, 256], P('tp', 'fsdp')
- new_right: float32 [4, 64, 6, 256, 256], P('tp', 'fsdp')
Inputs may be any that keep to these rules, and one draw needn't show every extreme that they name: `owner`: within each group of 128 consecutive blocks, no device owns more than 6 blocks, and some device owns exactly 6.
All inputs are finite; a program needn't handle non-finite values.
Results may differ from a plain program's by a relative error of at most 0.0003.
Values sent between devices are 32-bit elements; how exact they have to be, the bound alone decides.
A program may use at most 64 MiB of HBM per device.

v0:
```python
import jax
import jax.numpy as jnp
from jax import lax
from jax.sharding import PartitionSpec as P

PRECISE = lax.Precision.HIGHEST
ADAM_BETA = 0.95
STAT_BETA = 0.99
LEARN_RATE = 0.05
ADAM_EPS = 1e-08
NORM_EPS = 1e-06


def extent_mask(extents, row_ids, col_ids, half_size):
    row_live = row_ids[None, :] < extents[:, 0:1] * half_size
    col_live = col_ids[None, :] < extents[:, 1:2] * half_size
    return (row_live[:, :, None] & col_live[:, None, :]).astype(jnp.float32)


def slot_tables(owner_col, owners, load_max):
    column = owner_col.shape[0]
    onehot = (owner_col[:, None] == jnp.arange(owners, dtype=jnp.int32)[None, :]).astype(jnp.int32)
    slot_rank = jnp.sum((jnp.cumsum(onehot, axis=0) - onehot) * onehot, axis=1)
    flat_slot = owner_col * load_max + slot_rank
    slot_hits = flat_slot[:, None] == jnp.arange(owners * load_max, dtype=jnp.int32)[None, :]
    valid_slot = jnp.any(slot_hits, axis=0)
    block_index = jnp.sum(
        jnp.where(slot_hits, jnp.arange(column, dtype=jnp.int32)[:, None], 0), axis=0
    )
    return (flat_slot, valid_slot, block_index)


def refresh(slot_grad, left_old, right_old, left_inv, right_inv, slot_mask):
    left_prod = jnp.einsum("sij,skj->sik", slot_grad, slot_grad, precision=PRECISE)
    right_prod = jnp.einsum("sji,sjk->sik", slot_grad, slot_grad, precision=PRECISE)
    left_new = STAT_BETA * left_old + (1.0 - STAT_BETA) * left_prod
    right_new = STAT_BETA * right_old + (1.0 - STAT_BETA) * right_prod
    inner = jnp.einsum("sij,sjk->sik", left_inv.astype(jnp.float32), slot_grad, precision=PRECISE)
    precond = (
        jnp.einsum("sij,sjk->sik", inner, right_inv.astype(jnp.float32), precision=PRECISE)
        * slot_mask
    )
    return (left_new, right_new, precond)


def on_device(grads, weights, moments, left_stat, right_stat, left_root, right_root, owner, extent):
    owners = lax.axis_size("fsdp")
    my_index = lax.axis_index("fsdp")
    count_blocks, shard_rows, block_size = weights.shape
    load_max = left_stat.shape[2]
    half_size = block_size // 2
    summed = lax.psum_scatter(grads[0], "tp", scatter_dimension=0, tiled=True)
    row_ids = my_index * shard_rows + jnp.arange(shard_rows, dtype=jnp.int32)
    col_ids = jnp.arange(block_size, dtype=jnp.int32)
    summed = summed * extent_mask(extent, row_ids, col_ids, half_size)
    new_moment = ADAM_BETA * moments + (1.0 - ADAM_BETA) * summed * summed
    adam_dir = summed / (jnp.sqrt(new_moment) + ADAM_EPS)
    adam_part = jnp.sum(adam_dir * adam_dir, axis=(1, 2))
    flat_slot, valid_slot, block_index = slot_tables(owner, owners, load_max)
    adam_total = lax.psum(adam_part, "fsdp")
    outgoing = jnp.take(summed, block_index, axis=0) * valid_slot[:, None, None].astype(jnp.float32)
    outgoing = outgoing.reshape(owners, load_max, shard_rows, block_size)
    incoming = lax.all_to_all(outgoing, "fsdp", split_axis=0, concat_axis=2, tiled=True)[0]
    mine_index = lax.dynamic_slice_in_dim(block_index, my_index * load_max, load_max)
    mine_extent = jnp.take(extent, mine_index, axis=0)
    out_mask = extent_mask(mine_extent, col_ids, col_ids, half_size)
    left_new, right_new, precond = refresh(
        incoming, left_stat[0, 0], right_stat[0, 0], left_root[0, 0], right_root[0, 0], out_mask
    )
    prec_owner = jnp.sum(precond * precond, axis=(1, 2))
    spread_sq = jnp.broadcast_to(prec_owner[None, :, None], (1, load_max, owners))
    back_prec, back_sq = (
        lax.all_to_all(precond[None], "fsdp", split_axis=2, concat_axis=0, tiled=True),
        lax.all_to_all(spread_sq, "fsdp", split_axis=2, concat_axis=0, tiled=True),
    )
    home_prec = jnp.take(
        back_prec.reshape(owners * load_max, shard_rows, block_size), flat_slot, axis=0
    )
    prec_total = jnp.take(back_sq.reshape(owners * load_max), flat_slot)
    graft = jnp.sqrt(adam_total / (prec_total + NORM_EPS))
    new_weight = weights - LEARN_RATE * home_prec * graft[:, None, None]
    return (new_weight, new_moment, left_new[None, None], right_new[None, None])


def solution(mesh):
    in_specs = (
        P("tp", None, "fsdp", None),
        P("tp", "fsdp", None),
        P("tp", "fsdp", None),
        P("tp", "fsdp", None, None, None),
        P("tp", "fsdp", None, None, None),
        P("tp", "fsdp", None, None, None),
        P("tp", "fsdp", None, None, None),
        P("tp"),
        P("tp", None),
    )
    out_specs = (
        P("tp", "fsdp", None),
        P("tp", "fsdp", None),
        P("tp", "fsdp", None, None, None),
        P("tp", "fsdp", None, None, None),
    )
    return jax.shard_map(
        on_device, mesh=mesh, in_specs=in_specs, out_specs=out_specs, check_vma=False
    )
```

profile of v0, /device:TPU:1, one launch (start us, length us, event | category | flops | bytes accessed | tf_op | source)
XLA Modules:
  0.0 339.6 jit_solution(3484285128444985306)
XLA Ops:
  7.3 0.7 all-reduce.3.cloned.1.call-update
  9.0 0.6 dynamic-slice
  10.5 67.6 %all-reduce.3.cloned.1.call-done = f32[512,4,256]{2,1,0:T(4,128)} async-done(((f32[512,4,256]{2,1,0:T(4,128)}), f32[512,4,256]{2,1,0:T(4,128)}) %all-reduce.3.cloned.1.call-update) | async-done | bytes 2097168
  78.0 3.7 %multiply_reduce_fusion.1 = (f32[128]{0:T(128)S(1)}, f32[128,4,256]{2,1,0:T(4,128)}, f32[128,4,256]{2,1,0:T(4,128)S(1)}) fusion(f32[128,4,256]{2,1,0:T(4,128)S(1)} %copy-done.3, f32[512,4,256]{2,1,0:T(4,128)} %all-reduce.3.cloned.1.call-done, u32[]{:T(128)S(6)} %multiply.3, pred[128,256]{1,0:T(8,128)(4,1)S(1)} %iota_compare_fusion.1, ...), kind=kLoop, calls=%fused_computation.18 | loop fusion | flops 1310592 | bytes 2130948 | tf_op jit(solution)/shard_map/reduce_sum | solution.py:58
  81.7 2.5 gather_fusion.1
  84.2 2.3 select_multiply_fusion
  86.5 10.7 %all-to-all-start = ((f32[64,6,4,256]{3,2,1,0:T(4,128)}), f32[64,6,4,256]{3,2,1,0:T(4,128)S(1)}, u32[]{:S(2)}, u32[]{:S(2)}) async-start(f32[64,6,4,256]{3,2,1,0:T(4,128)} %select_multiply_fusion), calls=%async_computation | async-start | bytes 3145728 | tf_op jit(solution)/shard_map/all_to_all | solution.py:63
  98.3 38.7 %all-to-all-done = f32[64,6,4,256]{3,2,1,0:T(4,128)S(1)} async-done(((f32[64,6,4,256]{3,2,1,0:T(4,128)}), f32[64,6,4,256]{3,2,1,0:T(4,128)S(1)}, u32[]{:S(2)}, u32[]{:S(2)}) %all-to-all-start) | async-done | bytes 1572896 | tf_op jit(solution)/shard_map/all_to_all | solution.py:63
  137.0 1.4 copy.53
  138.4 1.9 squeeze.15
  140.3 1.0 fusion.3
  141.3 2.3 multiply_reduce_fusion
  143.6 0.6 broadcast_in_dim.88
  144.2 6.1 %all-to-all-start.2 = ((f32[1,6,64]{1,0,2:T(1,128)}), f32[1,6,64]{1,0,2:T(1,128)S(1)}, u32[]{:S(2)}, u32[]{:S(2)}) async-start(f32[1,6,64]{1,0,2:T(1,128)} %broadcast_in_dim.88), calls=%async_computation.2 | async-start | bytes 65536 | tf_op jit(solution)/shard_map/all_to_all | solution.py:74
  150.3 4.2 %copy.56 = f32[1,6,256,256]{3,0,1,2:T(1,128)} copy(f32[1,6,256,256]{3,2,1,0:T(8,128)} %bitcast.49) | data formatting | bytes 3145728 | tf_op jit(solution)/shard_map/broadcast_in_dim | solution.py:73
  154.5 5.0 %all-to-all-done.2 = f32[1,6,64]{1,0,2:T(1,128)S(1)} async-done(((f32[1,6,64]{1,0,2:T(1,128)}), f32[1,6,64]{1,0,2:T(1,128)S(1)}, u32[]{:S(2)}, u32[]{:S(2)}) %all-to-all-start.2) | async-done | bytes 1568 | tf_op jit(solution)/shard_map/all_to_all | solution.py:74
  159.5 5.5 %all-to-all-start.1 = ((f32[1,6,256,256]{3,0,1,2:T(1,128)}), f32[1,6,256,256]{3,0,1,2:T(1,128)}, u32[]{:S(2)}, u32[]{:S(2)}) async-start(f32[1,6,256,256]{3,0,1,2:T(1,128)} %copy.56), calls=%async_computation.1 | async-start | bytes 3145728 | tf_op jit(solution)/shard_map/all_to_all | solution.py:73
  165.1 152.9 %psum.7 = f32[128]{0:T(128)S(1)} all-reduce(f32[128]{0:T(128)S(1)} %get-tuple-element.8), channel_id=1, replica_groups=mesh['fsdp'=64,'tp'=4] {'fsdp'}, use_global_device_ids=true, to_apply=%region_6.7 | all-reduce | flops 128 | bytes 1024 | tf_op jit(solution)/shard_map/psum | solution.py:60
  318.0 4.5 %fusion.1 = f32[1,1,6,256,256]{4,3,2,1,0:T(8,128)} fusion(f32[1,1,6,256,256]{4,3,2,1,0:T(8,128)} %param.12, f32[6,256,256]{2,1,0:T(8,128)S(1)} %squeeze.15), kind=kOutput, calls=%fused_computation.7 | convolution fusion | flops 1209139200 | bytes 4718592 | tf_op jit(solution)/shard_map/sij,skj->sik/dot_general | solution.py:34
  322.5 3.9 %fusion = f32[1,1,6,256,256]{4,3,2,1,0:T(8,128)} fusion(f32[1,1,6,256,256]{4,3,2,1,0:T(8,128)S(1)} %copy-done.1, f32[6,256,256]{2,1,0:T(8,128)S(1)} %squeeze.15), kind=kOutput, calls=%fused_computation.5 | convolution fusion | flops 1209139200 | bytes 4718592 | tf_op jit(solution)/shard_map/sji,sjk->sik/dot_general | solution.py:35
  326.5 1.3 gather_fusion.3
  327.8 2.5 copy.57
  330.8 0.9 gather_fusion.2
  331.7 1.1 multiply_subtract_fusion
  (45 shorter events, 2.9 us)
Async XLA Ops:
  7.2 134.1 %copy-start = (bf16[1,1,6,256,256]{4,3,2,1,0:T(8,128)(2,1)S(1)}, bf16[1,1,6,256,256]{4,3,2,1,0:T(8,128)(2,1)}, u32[]{:S(2)}) copy-start(bf16[1,1,6,256,256]{4,3,2,1,0:T(8,128)(2,1)} %param.15) | copy-start | bytes 2359300
  7.2 1.8 copy-start.7
  7.2 0.8 copy-start.5
  7.2 3.0 copy-start.6
  7.2 70.8 %copy-start.3 = (f32[128,4,256]{2,1,0:T(4,128)S(1)}, f32[128,4,256]{2,1,0:T(4,128)}, u32[]{:S(2)}) copy-start(f32[128,4,256]{2,1,0:T(4,128)} %param.11) | copy-start | bytes 1572868
  7.2 70.8 %all-reduce.3.cloned.1.call-start = ((), (), s32[]{:S(2)}) async-start(), calls=%async_computation.3 | async-start | bytes 4194304
  86.5 50.5 %all-to-all-start = ((f32[64,6,4,256]{3,2,1,0:T(4,128)}), f32[64,6,4,256]{3,2,1,0:T(4,128)S(1)}, u32[]{:S(2)}, u32[]{:S(2)}) async-start(f32[64,6,4,256]{3,2,1,0:T(4,128)} %select_multiply_fusion), calls=%async_computation | async-start | bytes 3145728 | tf_op jit(solution)/shard_map/all_to_all | solution.py:63
  138.4 1.9 copy-start.2
  144.2 15.3 %all-to-all-start.2 = ((f32[1,6,64]{1,0,2:T(1,128)}), f32[1,6,64]{1,0,2:T(1,128)S(1)}, u32[]{:S(2)}, u32[]{:S(2)}) async-start(f32[1,6,64]{1,0,2:T(1,128)} %broadcast_in_dim.88), calls=%async_computation.2 | async-start | bytes 65536 | tf_op jit(solution)/shard_map/all_to_all | solution.py:74
  159.5 168.3 %all-to-all-start.1 = ((f32[1,6,256,256]{3,0,1,2:T(1,128)}), f32[1,6,256,256]{3,0,1,2:T(1,128)}, u32[]{:S(2)}, u32[]{:S(2)}) async-start(f32[1,6,256,256]{3,0,1,2:T(1,128)} %copy.56), calls=%async_computation.1 | async-start | bytes 3145728 | tf_op jit(solution)/shard_map/all_to_all | solution.py:73
  318.0 4.5 %copy-start.1 = (f32[1,1,6,256,256]{4,3,2,1,0:T(8,128)S(1)}, f32[1,1,6,256,256]{4,3,2,1,0:T(8,128)}, u32[]{:S(2)}) copy-start(f32[1,1,6,256,256]{4,3,2,1,0:T(8,128)} %param.13) | copy-start | bytes 4718596
  330.3 1.3 copy-start.4
Sparse Core Ops, SparseCore 0:
  10.4 67.5 all-reduce.2
where the time goes:
time: 340 us
  blocking collectives  153 us (45%)
  waiting for transfers between devices  112 us (33%)
  starting transfers between devices  22.4 us (7%)
  local copies, waits for them, and re-layouts  17.3 us (5%)
  between operations  15 us (4%)
  matrix products  11.6 us (3%)
  other arithmetic  8.41 us (2%)
    psum x1, blocking collectives, on_device(): adam_total = lax.psum(adam_part, 'fsdp')  153 us
    unnamed x2, waiting for transfers between devices  68.2 us
    all_to_all x1, waiting for transfers between devices, on_device(): lax.all_to_all(outgoing, 'fsdp', split_axis=0, concat_axis=2, tiled=True)[0]  38.7 us
    all_to_all x1, starting transfers between devices, on_device(): lax.all_to_all(outgoing, 'fsdp', split_axis=0, concat_axis=2, tiled=True)[0]  10.7 us
  transfers between devices with their start and end apart: 4, of which 3 were waited for; matrix products, arithmetic and copies ran while one was open for 5% of the time, Pallas kernels for 0%

commit v1 on v0

--- a/solution.py
+++ b/solution.py
@@ -57,7 +57,7 @@
     adam_dir = summed / (jnp.sqrt(new_moment) + ADAM_EPS)
     adam_part = jnp.sum(adam_dir * adam_dir, axis=(1, 2))
     flat_slot, valid_slot, block_index = slot_tables(owner, owners, load_max)
-    adam_total = lax.psum(adam_part, "fsdp")
+    adam_total = lax.all_gather(adam_part, "fsdp").sum(axis=0)
     outgoing = jnp.take(summed, block_index, axis=0) * valid_slot[:, None, None].astype(jnp.float32)
     outgoing = outgoing.reshape(owners, load_max, shard_rows, block_size)
     incoming = lax.all_to_all(outgoing, "fsdp", split_axis=0, concat_axis=2, tiled=True)[0]

time: 340 us -> 258 us (0.76)
  blocking collectives: 153 us -> 70.6 us
    psum x1 -> x0, blocking collectives: 153 us -> none  [on_device(): adam_total = lax.psum(adam_part, 'fsdp')]
    all_gather x0 -> x1, blocking collectives: none -> 70.6 us  [on_device(): adam_total = lax.all_gather(adam_part, 'fsdp').sum(axis=0)]
  transfers between devices with their start and end apart: 4 -> 4, of which waited for: 3 -> 3; matrix products, arithmetic and copies ran while one was open for 5% -> 7% of each run, Pallas kernels for 0% -> 0%
where the time goes in v1:
time: 258 us; the launch traced here: 257 us
  waiting for transfers between devices  112 us (43%)
  blocking collectives  70.6 us (27%)
  starting transfers between devices  22.4 us (9%)
  local copies, waits for them, and re-layouts  17.3 us (7%)
  between operations  15 us (6%)
  matrix products  11.6 us (4%)
  other arithmetic  8.5 us (3%)
    all_gather x1, blocking collectives, on_device(): adam_total = lax.all_gather(adam_part, 'fsdp').sum(axis=0)  70.6 us
    unnamed x2, waiting for transfers between devices  68.2 us
    all_to_all x1, waiting for transfers between devices, on_device(): lax.all_to_all(outgoing, 'fsdp', split_axis=0, concat_axis=2, tiled=True)[0]  38.7 us
    all_to_all x1, starting transfers between devices, on_device(): lax.all_to_all(outgoing, 'fsdp', split_axis=0, concat_axis=2, tiled=True)[0]  10.7 us
    all_to_all x1, starting transfers between devices, on_device(): lax.all_to_all(spread_sq, 'fsdp', split_axis=2, concat_axis=0, tiled=True)  6.12 us
    all_to_all x1, starting transfers between devices, on_device(): lax.all_to_all(precond[None], 'fsdp', split_axis=2, concat_axis=0, tiled=...  5.53 us
  transfers between devices with their start and end apart: 4, of which 3 were waited for; matrix products, arithmetic and copies ran while one was open for 7% of the time, Pallas kernels for 0%

profile of v1, /device:TPU:1, one launch (start us, length us, event | category | flops | bytes accessed | tf_op | source)
XLA Modules:
  0.0 257.4 jit_solution(16045657726888296485)
XLA Ops:
  7.3 0.7 all-reduce.3.cloned.1.call-update
  9.0 0.6 dynamic-slice
  10.5 67.6 %all-reduce.3.cloned.1.call-done = f32[512,4,256]{2,1,0:T(4,128)} async-done(((f32[512,4,256]{2,1,0:T(4,128)}), f32[512,4,256]{2,1,0:T(4,128)}) %all-reduce.3.cloned.1.call-update) | async-done | bytes 2097168
  78.0 3.7 %multiply_reduce_fusion.1 = (f32[128]{0:T(128)S(1)}, f32[128,4,256]{2,1,0:T(4,128)}, f32[128,4,256]{2,1,0:T(4,128)S(1)}) fusion(f32[128,4,256]{2,1,0:T(4,128)S(1)} %copy-done.3, f32[512,4,256]{2,1,0:T(4,128)} %all-reduce.3.cloned.1.call-done, u32[]{:T(128)S(6)} %multiply.3, pred[128,256]{1,0:T(8,128)(4,1)S(1)} %iota_compare_fusion.1, ...), kind=kLoop, calls=%fused_computation.18 | loop fusion | flops 1310592 | bytes 2130948 | tf_op jit(solution)/shard_map/reduce_sum | solution.py:58
  81.7 2.5 gather_fusion.1
  84.2 2.3 select_multiply_fusion
  86.5 10.7 %all-to-all-start = ((f32[64,6,4,256]{3,2,1,0:T(4,128)}), f32[64,6,4,256]{3,2,1,0:T(4,128)S(1)}, u32[]{:S(2)}, u32[]{:S(2)}) async-start(f32[64,6,4,256]{3,2,1,0:T(4,128)} %select_multiply_fusion), calls=%async_computation | async-start | bytes 3145728 | tf_op jit(solution)/shard_map/all_to_all | solution.py:63
  98.3 38.7 %all-to-all-done = f32[64,6,4,256]{3,2,1,0:T(4,128)S(1)} async-done(((f32[64,6,4,256]{3,2,1,0:T(4,128)}), f32[64,6,4,256]{3,2,1,0:T(4,128)S(1)}, u32[]{:S(2)}, u32[]{:S(2)}) %all-to-all-start) | async-done | bytes 1572896 | tf_op jit(solution)/shard_map/all_to_all | solution.py:63
  137.0 1.4 copy.53
  138.4 1.9 squeeze.15
  140.3 1.0 fusion.3
  141.3 2.3 multiply_reduce_fusion
  143.6 0.6 broadcast_in_dim.88
  144.2 6.1 %all-to-all-start.2 = ((f32[1,6,64]{1,0,2:T(1,128)}), f32[1,6,64]{1,0,2:T(1,128)S(1)}, u32[]{:S(2)}, u32[]{:S(2)}) async-start(f32[1,6,64]{1,0,2:T(1,128)} %broadcast_in_dim.88), calls=%async_computation.2 | async-start | bytes 65536 | tf_op jit(solution)/shard_map/all_to_all | solution.py:74
  150.3 4.2 %copy.56 = f32[1,6,256,256]{3,0,1,2:T(1,128)} copy(f32[1,6,256,256]{3,2,1,0:T(8,128)} %bitcast.50) | data formatting | bytes 3145728 | tf_op jit(solution)/shard_map/broadcast_in_dim | solution.py:73
  154.5 5.0 %all-to-all-done.2 = f32[1,6,64]{1,0,2:T(1,128)S(1)} async-done(((f32[1,6,64]{1,0,2:T(1,128)}), f32[1,6,64]{1,0,2:T(1,128)S(1)}, u32[]{:S(2)}, u32[]{:S(2)}) %all-to-all-start.2) | async-done | bytes 1568 | tf_op jit(solution)/shard_map/all_to_all | solution.py:74
  159.5 5.5 %all-to-all-start.1 = ((f32[1,6,256,256]{3,0,1,2:T(1,128)}), f32[1,6,256,256]{3,0,1,2:T(1,128)}, u32[]{:S(2)}, u32[]{:S(2)}) async-start(f32[1,6,256,256]{3,0,1,2:T(1,128)} %copy.56), calls=%async_computation.1 | async-start | bytes 3145728 | tf_op jit(solution)/shard_map/all_to_all | solution.py:73
  165.1 70.6 %all-gather.1 = f32[64,1,128]{2,1,0:T(1,128)S(1)} all-gather(f32[1,1,128]{2,1,0:T(1,128)S(1)} %bitcast.56), channel_id=2, replica_groups=mesh['fsdp'=64,'tp'=4] {'fsdp'}, dimensions={0}, use_global_device_ids=true | all-gather | bytes 33280 | tf_op jit(solution)/shard_map/all_gather | solution.py:60
  235.8 4.5 %fusion.1 = f32[1,1,6,256,256]{4,3,2,1,0:T(8,128)} fusion(f32[1,1,6,256,256]{4,3,2,1,0:T(8,128)} %param.12, f32[6,256,256]{2,1,0:T(8,128)S(1)} %squeeze.15), kind=kOutput, calls=%fused_computation.7 | convolution fusion | flops 1209139200 | bytes 4718592 | tf_op jit(solution)/shard_map/sij,skj->sik/dot_general | solution.py:34
  240.2 3.9 %fusion = f32[1,1,6,256,256]{4,3,2,1,0:T(8,128)} fusion(f32[1,1,6,256,256]{4,3,2,1,0:T(8,128)S(1)} %copy-done.1, f32[6,256,256]{2,1,0:T(8,128)S(1)} %squeeze.15), kind=kOutput, calls=%fused_computation.5 | convolution fusion | flops 1209139200 | bytes 4718592 | tf_op jit(solution)/shard_map/sji,sjk->sik/dot_general | solution.py:35
  244.3 1.3 gather_fusion.3
  245.6 2.5 copy.57
  248.5 0.9 gather_fusion.2
  249.4 1.1 multiply_subtract_fusion
  (46 shorter events, 2.9 us)
Async XLA Ops:
  7.2 134.1 %copy-start = (bf16[1,1,6,256,256]{4,3,2,1,0:T(8,128)(2,1)S(1)}, bf16[1,1,6,256,256]{4,3,2,1,0:T(8,128)(2,1)}, u32[]{:S(2)}) copy-start(bf16[1,1,6,256,256]{4,3,2,1,0:T(8,128)(2,1)} %param.15) | copy-start | bytes 2359300
  7.2 1.8 copy-start.7
  7.2 0.8 copy-start.5
  7.2 3.0 %copy-start.6 = (s32[128,2]{0,1:T(2,128)S(1)}, s32[128,2]{0,1:T(2,128)}, u32[]{:S(2)}) copy-start(s32[128,2]{0,1:T(2,128)} %param.17) | copy-start | bytes 3076
  7.2 70.8 %copy-start.3 = (f32[128,4,256]{2,1,0:T(4,128)S(1)}, f32[128,4,256]{2,1,0:T(4,128)}, u32[]{:S(2)}) copy-start(f32[128,4,256]{2,1,0:T(4,128)} %param.11) | copy-start | bytes 1572868
  7.2 70.8 %all-reduce.3.cloned.1.call-start = ((), (), s32[]{:S(2)}) async-start(), calls=%async_computation.3 | async-start | bytes 4194304
  86.5 50.5 %all-to-all-start = ((f32[64,6,4,256]{3,2,1,0:T(4,128)}), f32[64,6,4,256]{3,2,1,0:T(4,128)S(1)}, u32[]{:S(2)}, u32[]{:S(2)}) async-start(f32[64,6,4,256]{3,2,1,0:T(4,128)} %select_multiply_fusion), calls=%async_computation | async-start | bytes 3145728 | tf_op jit(solution)/shard_map/all_to_all | solution.py:63
  138.4 1.9 copy-start.2
  144.2 15.3 %all-to-all-start.2 = ((f32[1,6,64]{1,0,2:T(1,128)}), f32[1,6,64]{1,0,2:T(1,128)S(1)}, u32[]{:S(2)}, u32[]{:S(2)}) async-start(f32[1,6,64]{1,0,2:T(1,128)} %broadcast_in_dim.88), calls=%async_computation.2 | async-start | bytes 65536 | tf_op jit(solution)/shard_map/all_to_all | solution.py:74
  159.5 86.0 %all-to-all-start.1 = ((f32[1,6,256,256]{3,0,1,2:T(1,128)}), f32[1,6,256,256]{3,0,1,2:T(1,128)}, u32[]{:S(2)}, u32[]{:S(2)}) async-start(f32[1,6,256,256]{3,0,1,2:T(1,128)} %copy.56), calls=%async_computation.1 | async-start | bytes 3145728 | tf_op jit(solution)/shard_map/all_to_all | solution.py:73
  235.8 4.5 %copy-start.1 = (f32[1,1,6,256,256]{4,3,2,1,0:T(8,128)S(1)}, f32[1,1,6,256,256]{4,3,2,1,0:T(8,128)}, u32[]{:S(2)}) copy-start(f32[1,1,6,256,256]{4,3,2,1,0:T(8,128)} %param.13) | copy-start | bytes 4718596
  248.1 1.3 copy-start.4
Sparse Core Ops, SparseCore 0:
  10.4 67.5 all-reduce.2
